TPU v7x, 32 devices: a whole 2x2x4 slice. The times are simulated.
32 devices in a mesh: tm: 16 (over z, x, core), space: 2 (over y).
Axes of the slice: x: 2, y: 2, z: 4, core: 2. Of those that a mesh axis runs over, the one named last changes fastest.
Arguments:
- trajectory: bfloat16 [64, 64, 1024], P('tm', 'space'), may hold values from 0.19921875 to 0.8984375
- target: float32 [64, 1024], P('space'), may hold values from -6 to 6
- reaction: float32 [64, 1024], P('space'), may hold values from 0.0078125 to 0.3125
- guess: float32 [16, 64, 1024], P('tm', 'space'), may hold values from -6 to 6
Outputs:
- adjoint: float32 [64, 64, 1024], P('tm', 'space')
All inputs are finite; a program needn't handle non-finite values.
Results may differ from a plain program's by a relative error of at most 0.0003.
Values sent between devices are 32-bit elements; how exact they have to be, the bound alone decides.
A program may use at most 64 MiB of HBM per device.

v0:
```python
import jax
import jax.numpy as jnp
from jax import lax
from jax.sharding import PartitionSpec as P

DIFFUSION = 0.05


def extended_2(cells, sides, width):
    for axis, dim in sides:
        count = lax.axis_size(axis)
        ends = count - 1
        head = lax.slice_in_dim(cells, 0, width, axis=dim)
        tail = lax.slice_in_dim(cells, cells.shape[dim] - width, cells.shape[dim], axis=dim)
        cells = jnp.concatenate(
            [
                lax.ppermute(tail, axis, [(i, (i + 1) % count) for i in range(ends)]),
                cells,
                lax.ppermute(head, axis, [((i + 1) % count, i) for i in range(ends)]),
            ],
            axis=dim,
        )
    return cells


def passed_along(block, axis, distance):
    devices = range(lax.axis_size(axis))
    route = [(i - distance, i) for i in devices if i - distance in devices]
    return lax.ppermute(block, axis, route)


def entering(x, axis, combine, identity):
    peers, position = (lax.axis_size(axis), lax.axis_index(axis))
    everything = jax.tree.map(lambda part: lax.all_gather(part, axis), x)
    start = jax.tree.map(
        lambda part, zero: jnp.broadcast_to(jnp.asarray(zero, part.dtype), part.shape), x, identity
    )

    def turn(k, before):
        at = peers - 1 - k
        reached = at > position
        new = combine(before, jax.tree.map(lambda part: part[at], everything))
        return jax.tree.map(lambda a, b: jnp.where(reached, a, b), new, before)

    return lax.fori_loop(0, peers, turn, start)


def stencil(field, rate_field, source_field):
    center = field[:, 1:-1]
    neighbours = field[:, :-2] + field[:, 2:]
    padded = jnp.pad(center, ((0, 0), (0, 0), (1, 1)))
    neighbours = neighbours + padded[:, :, :-2] + padded[:, :, 2:]
    return center + DIFFUSION * (neighbours - 4.0 * center) + rate_field * center + source_field


def thin_step(field, rate_field, source_field):
    extended = extended_2(field, (("space", 1),), 1)
    return stencil(extended, rate_field, source_field)


def compose(earlier, latter):
    return (latter[0] * earlier[0], latter[0] * earlier[1] + latter[1])


def local(trajectory, target, reaction, guess):
    coarse = guess.shape[0]
    slab_steps, tile_rows, tile_cols = trajectory.shape
    factor = slab_steps // coarse
    n_time = lax.axis_size("tm")
    shaped = trajectory.astype(jnp.float32).reshape(coarse, factor, tile_rows, tile_cols)
    rate_terms = reaction[None, None] * (1.0 - 2.0 * shaped)
    sources = (shaped - target[None, None]) / float(slab_steps * n_time)
    coarse_rate = jnp.ones_like(guess)
    for i in range(factor):
        coarse_rate = coarse_rate * (1.0 + rate_terms[:, i])
    unit_field = jnp.ones((tile_rows, tile_cols), jnp.float32)
    zero_field = jnp.zeros((tile_rows, tile_cols), jnp.float32)
    running = unit_field
    suffixes = [None] * coarse
    j = 0
    running = coarse_rate[j] * running
    suffixes[j] = running
    whole_rate = suffixes[0]

    def upper_values(values):
        from_above = passed_along(values, "tm", -1)
        return jnp.concatenate([values[1:], from_above], 0)

    def relaxation(values, with_centre):
        field = upper_values(values)
        fine_vals = {}
        centre = None
        for i in range(factor - 1, 0, -1):
            field = thin_step(field, rate_terms[:, i], sources[:, i])
            fine_vals[i] = field
        if with_centre:
            centre = thin_step(field, rate_terms[:, 0], sources[:, 0])
        return (fine_vals, centre)

    _, cvalues = relaxation(guess, True)
    _, centre = relaxation(cvalues, True)
    residual = centre - cvalues
    offsets = [None] * coarse
    running = zero_field
    j = 0
    running = coarse_rate[j] * running + residual[j]
    offsets[j] = running
    whole_offset = offsets[0]
    _, incoming = entering((whole_rate, whole_offset), "tm", compose, (unit_field, zero_field))
    correction = jnp.stack([suffixes[0] * incoming + offsets[0]], 0)
    cvalues = cvalues + correction
    fine_vals, _ = relaxation(cvalues, False)
    stacked = jnp.stack([cvalues] + [fine_vals[i] for i in range(1, factor)], axis=1)
    return stacked.reshape(slab_steps, tile_rows, tile_cols)


def solution(mesh):
    in_specs = (P("tm", "space", None), P("space", None), P("space", None), P("tm", "space", None))
    out_specs = P("tm", "space", None)
    return jax.shard_map(local, mesh=mesh, in_specs=in_specs, out_specs=out_specs, check_vma=False)
```

profile of v0, /device:TPU:0, one launch (start us, length us, event | category | flops | bytes accessed | tf_op | source)
XLA Modules:
  0.0 214.7 jit_solution(12403516713171184434)
XLA Ops:
  7.8 2.2 %collective-permute-done = f32[1,32,1024]{2,1,0:T(8,128)S(1)} collective-permute-done((f32[1,32,1024]{2,1,0:T(8,128)}, f32[1,32,1024]{2,1,0:T(8,128)S(1)}, u32[]{:S(2)}, u32[]{:S(2)}) %collective-permute-start) | collective-permute-done | bytes 131104 | tf_op jit(solution)/shard_map/ppermute | solution.py:29
  10.0 4.9 %collective-permute-start.1 = (f32[1,1,1024]{2,1,0:T(1,128)S(1)}, f32[1,1,1024]{2,1,0:T(1,128)S(1)}, u32[]{:S(2)}, u32[]{:S(2)}) collective-permute-start(f32[1,1,1024]{2,1,0:T(1,128)S(1)} %get-tuple-element.191), channel_id=1, source_target_pairs={{0,1},{2,3},{4,5},{6,7},{8,9},{10,11},{12,13},{14,15},{16,17},{18,... | collective-permute-start | bytes 12296 | tf_op jit(solution)/shard_map/ppermute | solution.py:17
  17.4 3.0 %collective-permute-done.2 = f32[1,1,1024]{2,1,0:T(1,128)S(1)} collective-permute-done((f32[1,1,1024]{2,1,0:T(1,128)S(1)}, f32[1,1,1024]{2,1,0:T(1,128)S(1)}, u32[]{:S(2)}, u32[]{:S(2)}) %collective-permute-start.2) | collective-permute-done | bytes 4128 | tf_op jit(solution)/shard_map/ppermute | solution.py:19
  23.5 4.2 %collective-permute-done.4 = f32[1,1,1024]{2,1,0:T(1,128)S(1)} collective-permute-done((f32[1,1,1024]{2,1,0:T(1,128)S(1)}, f32[1,1,1024]{2,1,0:T(1,128)S(1)}, u32[]{:S(2)}, u32[]{:S(2)}) %collective-permute-start.4) | collective-permute-done | bytes 4128 | tf_op jit(solution)/shard_map/ppermute | solution.py:19
  27.9 1.7 collective-permute-start.5
  30.9 4.2 %collective-permute-done.6 = f32[1,1,1024]{2,1,0:T(1,128)S(1)} collective-permute-done((f32[1,1,1024]{2,1,0:T(1,128)S(1)}, f32[1,1,1024]{2,1,0:T(1,128)S(1)}, u32[]{:S(2)}, u32[]{:S(2)}) %collective-permute-start.6) | collective-permute-done | bytes 4128 | tf_op jit(solution)/shard_map/ppermute | solution.py:19
  38.2 4.2 %collective-permute-done.8 = f32[1,1,1024]{2,1,0:T(1,128)S(1)} collective-permute-done((f32[1,1,1024]{2,1,0:T(1,128)S(1)}, f32[1,1,1024]{2,1,0:T(1,128)S(1)}, u32[]{:S(2)}, u32[]{:S(2)}) %collective-permute-start.8) | collective-permute-done | bytes 4128 | tf_op jit(solution)/shard_map/ppermute | solution.py:19
  43.8 1.9 collective-permute-done.9
  48.7 4.2 %collective-permute-done.11 = f32[1,1,1024]{2,1,0:T(1,128)S(1)} collective-permute-done((f32[1,1,1024]{2,1,0:T(1,128)S(1)}, f32[1,1,1024]{2,1,0:T(1,128)S(1)}, u32[]{:S(2)}, u32[]{:S(2)}) %collective-permute-start.11) | collective-permute-done | bytes 4128 | tf_op jit(solution)/shard_map/ppermute | solution.py:19
  53.1 1.7 collective-permute-start.12
  56.1 4.2 %collective-permute-done.13 = f32[1,1,1024]{2,1,0:T(1,128)S(1)} collective-permute-done((f32[1,1,1024]{2,1,0:T(1,128)S(1)}, f32[1,1,1024]{2,1,0:T(1,128)S(1)}, u32[]{:S(2)}, u32[]{:S(2)}) %collective-permute-start.13) | collective-permute-done | bytes 4128 | tf_op jit(solution)/shard_map/ppermute | solution.py:19
  60.4 1.7 collective-permute-start.14
  63.4 4.2 %collective-permute-done.15 = f32[1,1,1024]{2,1,0:T(1,128)S(1)} collective-permute-done((f32[1,1,1024]{2,1,0:T(1,128)S(1)}, f32[1,1,1024]{2,1,0:T(1,128)S(1)}, u32[]{:S(2)}, u32[]{:S(2)}) %collective-permute-start.15) | collective-permute-done | bytes 4128 | tf_op jit(solution)/shard_map/ppermute | solution.py:19
  67.8 1.7 collective-permute-start.16
  70.7 4.2 %collective-permute-done.17 = f32[1,1,1024]{2,1,0:T(1,128)S(1)} collective-permute-done((f32[1,1,1024]{2,1,0:T(1,128)S(1)}, f32[1,1,1024]{2,1,0:T(1,128)S(1)}, u32[]{:S(2)}, u32[]{:S(2)}) %collective-permute-start.17) | collective-permute-done | bytes 4128 | tf_op jit(solution)/shard_map/ppermute | solution.py:19
  76.5 43.6 %all-gather.5.cloned.1.call-done = f32[16,32,1024]{2,1,0:T(8,128)} async-done(((f32[1,32,1024]{2,1,0:T(8,128)}), f32[16,32,1024]{2,1,0:T(8,128)}) %all-gather.5.cloned.1.call-update) | async-done | bytes 2097168 | tf_op jit(solution)/shard_map/all_gather | solution.py:34
  120.1 42.4 %all-gather.3.cloned.1.call-done = f32[16,32,1024]{2,1,0:T(8,128)} async-done(((f32[1,32,1024]{2,1,0:T(8,128)}), f32[16,32,1024]{2,1,0:T(8,128)}) %all-gather.3.cloned.1.call-update) | async-done | bytes 2097168 | tf_op jit(solution)/shard_map/all_gather | solution.py:34
  162.5 17.5 %while.16 = (s32[]{:T(128)}, f32[32,1024]{1,0:T(8,128)S(1)}, s32[]{:T(128)}, f32[16,32,1024]{2,1,0:T(8,128)}, f32[16,32,1024]{2,1,0:T(8,128)}, /*index=5*/s32[]{:T(128)}, s32[]{:T(128)}, s32[]{:T(128)}, s32[]{:T(128)}) while((s32[]{:T(128)}, f32[32,1024]{1,0:T(8,128)S(1)}, s32[]{:T(128)}, f32[16,32,1024]{2,1,0:T(8,128)}, ...), condition=%wide.region_1.2_spmd.clone, body=%wide.region_0.1_spmd.clone.sunk | while | flops 131080 | bytes 524459 | solution.py:45
  181.4 1.9 collective-permute-done.18
  183.3 3.4 %collective-permute-start.19 = (f32[1,1,1024]{2,1,0:T(1,128)S(1)}, f32[1,1,1024]{2,1,0:T(1,128)S(1)}, u32[]{:S(2)}, u32[]{:S(2)}) collective-permute-start(f32[1,1,1024]{2,1,0:T(1,128)S(1)} %get-tuple-element.175), channel_id=1, source_target_pairs={{0,1},{2,3},{4,5},{6,7},{8,9},{10,11},{12,13},{14,15},{16,17},{18,... | collective-permute-start | bytes 12296 | tf_op jit(solution)/shard_map/ppermute | solution.py:17
  188.0 4.2 %collective-permute-done.20 = f32[1,1,1024]{2,1,0:T(1,128)S(1)} collective-permute-done((f32[1,1,1024]{2,1,0:T(1,128)S(1)}, f32[1,1,1024]{2,1,0:T(1,128)S(1)}, u32[]{:S(2)}, u32[]{:S(2)}) %collective-permute-start.20) | collective-permute-done | bytes 4128 | tf_op jit(solution)/shard_map/ppermute | solution.py:19
  195.4 4.2 %collective-permute-done.22 = f32[1,1,1024]{2,1,0:T(1,128)S(1)} collective-permute-done((f32[1,1,1024]{2,1,0:T(1,128)S(1)}, f32[1,1,1024]{2,1,0:T(1,128)S(1)}, u32[]{:S(2)}, u32[]{:S(2)}) %collective-permute-start.22) | collective-permute-done | bytes 4128 | tf_op jit(solution)/shard_map/ppermute | solution.py:19
  199.7 1.7 collective-permute-start.23
  202.7 4.2 %collective-permute-done.24 = f32[1,1,1024]{2,1,0:T(1,128)S(1)} collective-permute-done((f32[1,1,1024]{2,1,0:T(1,128)S(1)}, f32[1,1,1024]{2,1,0:T(1,128)S(1)}, u32[]{:S(2)}, u32[]{:S(2)}) %collective-permute-start.24) | collective-permute-done | bytes 4128 | tf_op jit(solution)/shard_map/ppermute | solution.py:19
  (75 shorter events, 47.1 us)
Async XLA Ops:
  6.5 113.6 %all-gather.5.cloned.1.call-start = ((), (), s32[]{:S(2)}) async-start(), calls=%async_computation.1 | async-start | bytes 2228224 | tf_op jit(solution)/shard_map/all_gather | solution.py:34
  6.5 3.4 %collective-permute-start = (f32[1,32,1024]{2,1,0:T(8,128)}, f32[1,32,1024]{2,1,0:T(8,128)S(1)}, u32[]{:S(2)}, u32[]{:S(2)}) collective-permute-start(f32[1,32,1024]{2,1,0:T(8,128)} %param.9), channel_id=1, source_target_pairs={{2,0},{4,2},{6,4},{8,6},{10,8},{12,10},{14,12},{16,14},{18,16},{20... | collective-permute-start | bytes 393224 | tf_op jit(solution)/shard_map/ppermute | solution.py:29
  10.0 7.4 %collective-permute-start.1 = (f32[1,1,1024]{2,1,0:T(1,128)S(1)}, f32[1,1,1024]{2,1,0:T(1,128)S(1)}, u32[]{:S(2)}, u32[]{:S(2)}) collective-permute-start(f32[1,1,1024]{2,1,0:T(1,128)S(1)} %get-tuple-element.191), channel_id=1, source_target_pairs={{0,1},{2,3},{4,5},{6,7},{8,9},{10,11},{12,13},{14,15},{16,17},{18,... | collective-permute-start | bytes 12296 | tf_op jit(solution)/shard_map/ppermute | solution.py:17
  14.9 5.5 %collective-permute-start.2 = (f32[1,1,1024]{2,1,0:T(1,128)S(1)}, f32[1,1,1024]{2,1,0:T(1,128)S(1)}, u32[]{:S(2)}, u32[]{:S(2)}) collective-permute-start(f32[1,1,1024]{2,1,0:T(1,128)S(1)} %get-tuple-element.192), channel_id=1, source_target_pairs={{1,0},{3,2},{5,4},{7,6},{9,8},{11,10},{13,12},{15,14},{17,16},{19,... | collective-permute-start | bytes 12296 | tf_op jit(solution)/shard_map/ppermute | solution.py:19
  20.6 3.0 %collective-permute-start.3 = (f32[1,1,1024]{2,1,0:T(1,128)S(1)}, f32[1,1,1024]{2,1,0:T(1,128)S(1)}, u32[]{:S(2)}, u32[]{:S(2)}) collective-permute-start(f32[1,1,1024]{2,1,0:T(1,128)S(1)} %get-tuple-element.189), channel_id=1, source_target_pairs={{0,1},{2,3},{4,5},{6,7},{8,9},{10,11},{12,13},{14,15},{16,17},{18,... | collective-permute-start | bytes 12296 | tf_op jit(solution)/shard_map/ppermute | solution.py:17
  22.2 5.5 %collective-permute-start.4 = (f32[1,1,1024]{2,1,0:T(1,128)S(1)}, f32[1,1,1024]{2,1,0:T(1,128)S(1)}, u32[]{:S(2)}, u32[]{:S(2)}) collective-permute-start(f32[1,1,1024]{2,1,0:T(1,128)S(1)} %get-tuple-element.190), channel_id=1, source_target_pairs={{1,0},{3,2},{5,4},{7,6},{9,8},{11,10},{13,12},{15,14},{17,16},{19,... | collective-permute-start | bytes 12296 | tf_op jit(solution)/shard_map/ppermute | solution.py:19
  27.9 3.0 %collective-permute-start.5 = (f32[1,1,1024]{2,1,0:T(1,128)S(1)}, f32[1,1,1024]{2,1,0:T(1,128)S(1)}, u32[]{:S(2)}, u32[]{:S(2)}) collective-permute-start(f32[1,1,1024]{2,1,0:T(1,128)S(1)} %get-tuple-element.187), channel_id=1, source_target_pairs={{0,1},{2,3},{4,5},{6,7},{8,9},{10,11},{12,13},{14,15},{16,17},{18,... | collective-permute-start | bytes 12296 | tf_op jit(solution)/shard_map/ppermute | solution.py:17
  29.5 5.5 %collective-permute-start.6 = (f32[1,1,1024]{2,1,0:T(1,128)S(1)}, f32[1,1,1024]{2,1,0:T(1,128)S(1)}, u32[]{:S(2)}, u32[]{:S(2)}) collective-permute-start(f32[1,1,1024]{2,1,0:T(1,128)S(1)} %get-tuple-element.188), channel_id=1, source_target_pairs={{1,0},{3,2},{5,4},{7,6},{9,8},{11,10},{13,12},{15,14},{17,16},{19,... | collective-permute-start | bytes 12296 | tf_op jit(solution)/shard_map/ppermute | solution.py:19
  36.9 5.5 %collective-permute-start.8 = (f32[1,1,1024]{2,1,0:T(1,128)S(1)}, f32[1,1,1024]{2,1,0:T(1,128)S(1)}, u32[]{:S(2)}, u32[]{:S(2)}) collective-permute-start(f32[1,1,1024]{2,1,0:T(1,128)S(1)} %get-tuple-element.186), channel_id=1, source_target_pairs={{1,0},{3,2},{5,4},{7,6},{9,8},{11,10},{13,12},{15,14},{17,16},{19,... | collective-permute-start | bytes 12296 | tf_op jit(solution)/shard_map/ppermute | solution.py:19
  42.5 3.2 %collective-permute-start.9 = (f32[1,32,1024]{2,1,0:T(8,128)S(1)}, f32[1,32,1024]{2,1,0:T(8,128)S(1)}, u32[]{:S(2)}, u32[]{:S(2)}) collective-permute-start(f32[1,32,1024]{2,1,0:T(8,128)S(1)} %fusion.33), channel_id=1, source_target_pairs={{2,0},{4,2},{6,4},{8,6},{10,8},{12,10},{14,12},{16,14},{18,16},{20... | collective-permute-start | bytes 393224 | tf_op jit(solution)/shard_map/ppermute | solution.py:29
  47.4 5.5 %collective-permute-start.11 = (f32[1,1,1024]{2,1,0:T(1,128)S(1)}, f32[1,1,1024]{2,1,0:T(1,128)S(1)}, u32[]{:S(2)}, u32[]{:S(2)}) collective-permute-start(f32[1,1,1024]{2,1,0:T(1,128)S(1)} %get-tuple-element.184), channel_id=1, source_target_pairs={{1,0},{3,2},{5,4},{7,6},{9,8},{11,10},{13,12},{15,14},{17,16},{19,... | collective-permute-start | bytes 12296 | tf_op jit(solution)/shard_map/ppermute | solution.py:19
  53.1 3.0 %collective-permute-start.12 = (f32[1,1,1024]{2,1,0:T(1,128)S(1)}, f32[1,1,1024]{2,1,0:T(1,128)S(1)}, u32[]{:S(2)}, u32[]{:S(2)}) collective-permute-start(f32[1,1,1024]{2,1,0:T(1,128)S(1)} %get-tuple-element.181), channel_id=1, source_target_pairs={{0,1},{2,3},{4,5},{6,7},{8,9},{10,11},{12,13},{14,15},{16,17},{18,... | collective-permute-start | bytes 12296 | tf_op jit(solution)/shard_map/ppermute | solution.py:17
  54.8 5.5 %collective-permute-start.13 = (f32[1,1,1024]{2,1,0:T(1,128)S(1)}, f32[1,1,1024]{2,1,0:T(1,128)S(1)}, u32[]{:S(2)}, u32[]{:S(2)}) collective-permute-start(f32[1,1,1024]{2,1,0:T(1,128)S(1)} %get-tuple-element.182), channel_id=1, source_target_pairs={{1,0},{3,2},{5,4},{7,6},{9,8},{11,10},{13,12},{15,14},{17,16},{19,... | collective-permute-start | bytes 12296 | tf_op jit(solution)/shard_map/ppermute | solution.py:19
  60.4 3.0 %collective-permute-start.14 = (f32[1,1,1024]{2,1,0:T(1,128)S(1)}, f32[1,1,1024]{2,1,0:T(1,128)S(1)}, u32[]{:S(2)}, u32[]{:S(2)}) collective-permute-start(f32[1,1,1024]{2,1,0:T(1,128)S(1)} %get-tuple-element.179), channel_id=1, source_target_pairs={{0,1},{2,3},{4,5},{6,7},{8,9},{10,11},{12,13},{14,15},{16,17},{18,... | collective-permute-start | bytes 12296 | tf_op jit(solution)/shard_map/ppermute | solution.py:17
  62.1 5.5 %collective-permute-start.15 = (f32[1,1,1024]{2,1,0:T(1,128)S(1)}, f32[1,1,1024]{2,1,0:T(1,128)S(1)}, u32[]{:S(2)}, u32[]{:S(2)}) collective-permute-start(f32[1,1,1024]{2,1,0:T(1,128)S(1)} %get-tuple-element.180), channel_id=1, source_target_pairs={{1,0},{3,2},{5,4},{7,6},{9,8},{11,10},{13,12},{15,14},{17,16},{19,... | collective-permute-start | bytes 12296 | tf_op jit(solution)/shard_map/ppermute | solution.py:19
  67.8 3.0 %collective-permute-start.16 = (f32[1,1,1024]{2,1,0:T(1,128)S(1)}, f32[1,1,1024]{2,1,0:T(1,128)S(1)}, u32[]{:S(2)}, u32[]{:S(2)}) collective-permute-start(f32[1,1,1024]{2,1,0:T(1,128)S(1)} %get-tuple-element.177), channel_id=1, source_target_pairs={{0,1},{2,3},{4,5},{6,7},{8,9},{10,11},{12,13},{14,15},{16,17},{18,... | collective-permute-start | bytes 12296 | tf_op jit(solution)/shard_map/ppermute | solution.py:17
  69.4 5.5 %collective-permute-start.17 = (f32[1,1,1024]{2,1,0:T(1,128)S(1)}, f32[1,1,1024]{2,1,0:T(1,128)S(1)}, u32[]{:S(2)}, u32[]{:S(2)}) collective-permute-start(f32[1,1,1024]{2,1,0:T(1,128)S(1)} %get-tuple-element.178), channel_id=1, source_target_pairs={{1,0},{3,2},{5,4},{7,6},{9,8},{11,10},{13,12},{15,14},{17,16},{19,... | collective-permute-start | bytes 12296 | tf_op jit(solution)/shard_map/ppermute | solution.py:19
  75.8 86.7 %all-gather.3.cloned.1.call-start = ((), (), s32[]{:S(2)}) async-start(), calls=%async_computation | async-start | bytes 2228224 | tf_op jit(solution)/shard_map/all_gather | solution.py:34
  180.1 3.2 %collective-permute-start.18 = (f32[1,32,1024]{2,1,0:T(8,128)S(1)}, f32[1,32,1024]{2,1,0:T(8,128)S(1)}, u32[]{:S(2)}, u32[]{:S(2)}) collective-permute-start(f32[1,32,1024]{2,1,0:T(8,128)S(1)} %bitcast_add_fusion.1), channel_id=1, source_target_pairs={{2,0},{4,2},{6,4},{8,6},{10,8},{12,10},{14,12},{16,14},{18,16},{20... | collective-permute-start | bytes 393224 | tf_op jit(solution)/shard_map/ppermute | solution.py:29
  183.3 4.7 %collective-permute-start.19 = (f32[1,1,1024]{2,1,0:T(1,128)S(1)}, f32[1,1,1024]{2,1,0:T(1,128)S(1)}, u32[]{:S(2)}, u32[]{:S(2)}) collective-permute-start(f32[1,1,1024]{2,1,0:T(1,128)S(1)} %get-tuple-element.175), channel_id=1, source_target_pairs={{0,1},{2,3},{4,5},{6,7},{8,9},{10,11},{12,13},{14,15},{16,17},{18,... | collective-permute-start | bytes 12296 | tf_op jit(solution)/shard_map/ppermute | solution.py:17
  186.7 5.5 %collective-permute-start.20 = (f32[1,1,1024]{2,1,0:T(1,128)S(1)}, f32[1,1,1024]{2,1,0:T(1,128)S(1)}, u32[]{:S(2)}, u32[]{:S(2)}) collective-permute-start(f32[1,1,1024]{2,1,0:T(1,128)S(1)} %get-tuple-element.176), channel_id=1, source_target_pairs={{1,0},{3,2},{5,4},{7,6},{9,8},{11,10},{13,12},{15,14},{17,16},{19,... | collective-permute-start | bytes 12296 | tf_op jit(solution)/shard_map/ppermute | solution.py:19
  194.0 5.5 %collective-permute-start.22 = (f32[1,1,1024]{2,1,0:T(1,128)S(1)}, f32[1,1,1024]{2,1,0:T(1,128)S(1)}, u32[]{:S(2)}, u32[]{:S(2)}) collective-permute-start(f32[1,1,1024]{2,1,0:T(1,128)S(1)} %get-tuple-element.174), channel_id=1, source_target_pairs={{1,0},{3,2},{5,4},{7,6},{9,8},{11,10},{13,12},{15,14},{17,16},{19,... | collective-permute-start | bytes 12296 | tf_op jit(solution)/shard_map/ppermute | solution.py:19
  199.7 3.0 %collective-permute-start.23 = (f32[1,1,1024]{2,1,0:T(1,128)S(1)}, f32[1,1,1024]{2,1,0:T(1,128)S(1)}, u32[]{:S(2)}, u32[]{:S(2)}) collective-permute-start(f32[1,1,1024]{2,1,0:T(1,128)S(1)} %get-tuple-element.171), channel_id=1, source_target_pairs={{0,1},{2,3},{4,5},{6,7},{8,9},{10,11},{12,13},{14,15},{16,17},{18,... | collective-permute-start | bytes 12296 | tf_op jit(solution)/shard_map/ppermute | solution.py:17
  201.4 5.5 %collective-permute-start.24 = (f32[1,1,1024]{2,1,0:T(1,128)S(1)}, f32[1,1,1024]{2,1,0:T(1,128)S(1)}, u32[]{:S(2)}, u32[]{:S(2)}) collective-permute-start(f32[1,1,1024]{2,1,0:T(1,128)S(1)} %get-tuple-element.172), channel_id=1, source_target_pairs={{1,0},{3,2},{5,4},{7,6},{9,8},{11,10},{13,12},{15,14},{17,16},{19,... | collective-permute-start | bytes 12296 | tf_op jit(solution)/shard_map/ppermute | solution.py:19
  (3 other events, 8.9 us)
Sparse Core Ops, SparseCore 0:
  75.9 44.1 all-gather.4
  122.3 40.1 all-gather.2
where the time goes:
time: 216 us; the launch traced here: 215 us
  waiting for transfers between devices  138 us (64%)
  starting transfers between devices  41.3 us (19%)
  other arithmetic  21.4 us (10%)
  between operations  13.8 us (6%)
    all_gather x2, waiting for transfers between devices, entering(): everything = jax.tree.map(lambda part: lax.all_gather(part, axis), x)  85.9 us
    ppermute x11, waiting for transfers between devices, extended_2(): lax.ppermute(head, axis, [((i + 1) % count, i) for i in range(ends)])  44.9 us
    ppermute x11, starting transfers between devices, extended_2(): lax.ppermute(tail, axis, [(i, (i + 1) % count) for i in range(ends)])  23.1 us
    select_n x16, other arithmetic, turn(): return jax.tree.map(lambda a, b: jnp.where(reached, a, b), new, before)  17.1 us
    ppermute x11, starting transfers between devices, extended_2(): lax.ppermute(head, axis, [((i + 1) % count, i) for i in range(ends)])  14.2 us
    ppermute x3, waiting for transfers between devices, passed_along(): return lax.ppermute(block, axis, route)  6.04 us
  transfers between devices with their start and end apart: 27, of which 16 were waited for; matrix products, arithmetic and copies ran while one was open for 1% of the time, Pallas kernels for 0%

commit v1 on v0

v1 whole, which is shorter than its diff:
```python
import functools
import jax
import jax.numpy as jnp
from jax import lax
from jax.experimental import pallas as pl
from jax.experimental.pallas import tpu as pltpu
from jax.sharding import PartitionSpec as P

DIFFUSION = 0.05
MESH = pl.DeviceIdType.MESH
EDGE = 8


def group_size(count, cols):
    best = 1
    for d in range(1, count + 1):
        if d * d <= count and count % d == 0 and cols % (128 * d) == 0:
            best = d
    return best


def kernel(
    n, ns, size, steps,
    traj_in, targ_in, reac_in, guess_in, out_ref,
    traj, targ, reac, coef, src, spread, arate, x0, x0h, x1, x1h, packs, packr,
    c1, res, ga, gr, ppa, pp, rpa, rp, es, e, eh, fine,
    load_sem, out_sem, send_sem, recv_sem,
):
    factor, rows, cols = traj.shape
    quarter = cols // size
    groups = n // size
    ext = rows + EDGE
    half = EDGE // 2
    t, s = lax.axis_index("tm"), lax.axis_index("space")
    m, g = lax.rem(t, size), lax.div(t, size)
    base = g * size
    has_up, has_down = s > 0, s < ns - 1
    has_prev, has_next = t > 0, t < n - 1
    both = jnp.logical_and

    loads = [
        pltpu.make_async_copy(a, b, load_sem.at[i])
        for i, (a, b) in enumerate([(traj_in, traj), (reac_in, reac), (targ_in, targ)])
    ]
    for copy in loads:
        copy.start()

    def clear(condition, *refs):
        @pl.when(condition)
        def _():
            for ref in refs:
                ref[...] = jnp.zeros(ref.shape, ref.dtype)

    clear(jnp.logical_not(has_next), x0, x1)
    clear(jnp.logical_not(both(has_next, has_down)), x0h.at[0], x1h.at[0])
    clear(jnp.logical_not(both(has_next, has_up)), x0h.at[1], x1h.at[1])
    clear(jnp.logical_not(has_down), eh.at[0], *[packr.at[i, 0] for i in range(factor - 1)])
    clear(jnp.logical_not(has_up), eh.at[1], *[packr.at[i, 1] for i in range(factor - 1)])
    for d in range(1, groups):
        clear(g + d >= groups, rp.at[d], rpa.at[d])

    barrier = pltpu.get_barrier_semaphore()
    greeted = jnp.int32(0)

    def greet(condition, device):
        @pl.when(condition)
        def _():
            pl.semaphore_signal(barrier, inc=1, device_id=device, device_id_type=MESH)

        return jnp.where(condition, 1, 0).astype(jnp.int32)

    always = s >= 0
    for ds, here in ((0, always), (-1, has_up), (1, has_down)):
        greeted += greet(both(has_prev, here), (t - 1, s + ds))
        greeted += greet(both(has_next, here), (t + 1, s + ds))
        if ds:
            greeted += greet(here, (t, s + ds))
        for d in range(1, size):
            greeted += greet(here, (base + lax.rem(m + d, size), s + ds))
    for d in range(1, groups):
        greeted += greet(g - d >= 0, (t - d * size, s))
        greeted += greet(g + d < groups, (t + d * size, s))

    counter = [0]
    sent = []

    class Move:
        def __init__(self, source, target, device, sends, receives):
            k = counter[0]
            counter[0] += 1
            self.copy = pltpu.make_async_remote_copy(
                src_ref=source, dst_ref=target, send_sem=send_sem.at[k],
                recv_sem=recv_sem.at[k], device_id=device, device_id_type=MESH,
            )
            self.sends, self.receives = sends, receives
            sent.append(self)

        def start(self):
            pl.when(self.sends)(lambda: self.copy.start())

        def landed(self):
            pl.when(self.receives)(lambda: self.copy.wait_recv())

        def left(self):
            pl.when(self.sends)(lambda: self.copy.wait_send())

    top, bottom = pl.ds(0, EDGE), pl.ds(rows - EDGE, EDGE)

    def to_previous(source, x, xh):
        return [
            Move(source.at[top], xh.at[0], (t - 1, s - 1), both(has_prev, has_up), both(has_next, has_down)),
            Move(source.at[bottom], xh.at[1], (t - 1, s + 1), both(has_prev, has_down), both(has_next, has_up)),
            Move(source, x, (t - 1, s), has_prev, has_next),
        ]

    def part(k):
        return pl.ds(pl.multiple_of(k * quarter, quarter), quarter)

    def member(d):
        return lax.rem(m + d, size)

    pl.semaphore_wait(barrier, greeted)
    first = to_previous(guess_in.at[0], x0, x0h)
    for move in first:
        move.start()

    for copy in loads:
        copy.wait()

    sub = lax.broadcasted_iota(jnp.int32, (EDGE, cols), 0) < half

    def halo(from_below, from_above):
        return jnp.where(sub, from_below, from_above)

    reaction = reac[...]
    target = targ[...]
    rates = [None] * factor
    strips = []
    for i in range(factor - 1, -1, -1):
        state = traj[i].astype(jnp.float32)
        rates[i] = reaction * (1.0 - 2.0 * state)
        c = (1.0 - 4.0 * DIFFUSION) + rates[i]
        q = (state - target) * (1.0 / steps)
        coef[i, :rows] = c
        src[i, :rows] = q
        if i:
            packs[i - 1, 0] = jnp.where(sub, c[:EDGE], pltpu.roll(q[:EDGE], half, 0))
            packs[i - 1, 1] = jnp.where(sub, pltpu.roll(q[rows - EDGE :], half, 0), c[rows - EDGE :])
            pair = [
                Move(packs.at[i - 1, 0], packr.at[i - 1, 0], (t, s - 1), has_up, has_down),
                Move(packs.at[i - 1, 1], packr.at[i - 1, 1], (t, s + 1), has_down, has_up),
            ]
            for move in pair:
                move.start()
            strips.append((i, pair))
        else:
            coef[i, rows:] = jnp.zeros((EDGE, cols), jnp.float32)
            src[i, rows:] = jnp.zeros((EDGE, cols), jnp.float32)
    product = 1.0 + rates[0]
    for i in range(1, factor):
        product = product * (1.0 + rates[i])
    arate[...] = product
    below = jnp.where(has_down, DIFFUSION, 0.0).astype(jnp.float32)
    above = jnp.where(has_up, DIFFUSION, 0.0).astype(jnp.float32)
    spread[...] = jnp.where(sub, below, above)

    for i, pair in strips:
        for move in pair:
            move.landed()
        b, a = packr[i - 1, 0], packr[i - 1, 1]
        coef[i, rows:] = halo(b, a)
        src[i, rows:] = pltpu.roll(halo(a, b), half, 0)

    column = lax.broadcasted_iota(jnp.int32, (ext, cols), 1)

    def advance(v, i):
        around = pltpu.roll(v, 1, 0) + pltpu.roll(v, ext - 1, 0)
        around = around + jnp.where(column == 0, 0.0, pltpu.roll(v, 1, 1))
        around = around + jnp.where(column == cols - 1, 0.0, pltpu.roll(v, cols - 1, 1))
        scaled = jnp.concatenate([DIFFUSION * around[:rows], spread[...] * around[rows:]], 0)
        return coef[i] * v + scaled + src[i]

    def relax(v):
        for i in range(factor - 1, -1, -1):
            v = advance(v, i)
        return v[:rows]

    for move in first:
        move.landed()
    centre = relax(jnp.concatenate([x0[...], halo(x0h[0], x0h[1])], 0))
    c1[...] = centre
    second = to_previous(c1, x1, x1h)
    for move in second:
        move.start()

    def transpose(source, target):
        moves = [
            Move(source.at[:, part(member(d))], target.at[m], (base + member(d), s), always, always)
            for d in range(1, size)
        ]
        for move in moves:
            move.start()
        target[m] = source[:, part(m)]
        return moves

    a_moves = transpose(arate, ga)

    for move in second:
        move.landed()
    centre = relax(jnp.concatenate([x1[...], halo(x1h[0], x1h[1])], 0))
    res[...] = centre - c1[...]
    r_moves = transpose(res, gr)

    def to_lower(source, target):
        moves = [
            Move(source, target.at[d], (t - d * size, s), g - d >= 0, g + d < groups)
            for d in range(groups - 1, 0, -1)
        ]
        for move in moves:
            move.start()
        return moves

    for move in a_moves:
        move.landed()
    value = ga[0]
    for k in range(1, size):
        value = value * ga[k]
    ppa[...] = value
    pa_moves = to_lower(ppa, rpa)

    for move in r_moves:
        move.landed()
    value = gr[size - 1]
    for k in range(size - 2, -1, -1):
        value = ga[k] * value + gr[k]
    pp[...] = value
    p_moves = to_lower(pp, rp)
    for move in pa_moves:
        move.landed()
    for move in p_moves:
        move.landed()

    value = rp[groups - 1]
    for d in range(groups - 2, 0, -1):
        value = rp[d] + rpa[d] * value
    es[size - 1] = value
    for k in range(size - 1, 0, -1):
        value = ga[k] * value + gr[k]
        es[k - 1] = value
    e_moves = []
    for d in range(size - 1, -1, -1):
        k = member(d)
        to = base + k
        moves = [
            Move(es.at[k, top], eh.at[0, :, part(m)], (to, s - 1), has_up, has_down),
            Move(es.at[k, bottom], eh.at[1, :, part(m)], (to, s + 1), has_down, has_up),
        ]
        if d:
            moves.append(Move(es.at[k], e.at[:, part(m)], (to, s), always, always))
        for move in moves:
            move.start()
        e_moves += moves
    e[:, part(m)] = es[m]
    for move in e_moves:
        move.landed()

    entering = e[...]
    fine[0] = c1[...] + (arate[...] * entering + res[...])
    outs = [pltpu.make_async_copy(fine.at[i], out_ref.at[i], out_sem.at[i]) for i in range(factor)]
    outs[0].start()
    v = jnp.concatenate([x1[...] + entering, halo(x1h[0], x1h[1]) + halo(eh[0], eh[1])], 0)
    for i in range(factor - 1, 0, -1):
        v = advance(v, i)
        fine[i] = v[:rows]
        outs[i].start()
    for copy in outs:
        copy.wait()
    for move in sent:
        move.left()


def local(trajectory, target, reaction, guess):
    factor, rows, cols = trajectory.shape
    assert guess.shape[0] == 1
    n, ns = lax.axis_size("tm"), lax.axis_size("space")
    size = group_size(n, cols)
    groups = n // size
    quarter = cols // size
    ext = rows + EDGE
    copies = 6 + 2 * (factor - 1) + 2 * (size - 1) + 2 * (groups - 1) + 3 * size - 1
    f32 = jnp.float32
    vmem = lambda *shape: pltpu.VMEM(shape, f32)
    anywhere = pl.BlockSpec(memory_space=pl.ANY)
    return pl.pallas_call(
        functools.partial(kernel, n, ns, size, float(factor * n)),
        out_shape=jax.ShapeDtypeStruct((factor, rows, cols), f32),
        in_specs=[anywhere] * 4,
        out_specs=anywhere,
        scratch_shapes=[
            pltpu.VMEM((factor, rows, cols), trajectory.dtype),
            vmem(rows, cols), vmem(rows, cols),
            vmem(factor, ext, cols), vmem(factor, ext, cols), vmem(EDGE, cols),
            vmem(rows, cols),
            vmem(rows, cols), vmem(2, EDGE, cols), vmem(rows, cols), vmem(2, EDGE, cols),
            vmem(factor - 1, 2, EDGE, cols), vmem(factor - 1, 2, EDGE, cols),
            vmem(rows, cols), vmem(rows, cols),
            vmem(size, rows, quarter), vmem(size, rows, quarter),
            vmem(rows, quarter), vmem(rows, quarter),
            vmem(groups, rows, quarter), vmem(groups, rows, quarter),
            vmem(size, rows, quarter), vmem(rows, cols), vmem(2, EDGE, cols),
            vmem(factor, rows, cols),
            pltpu.SemaphoreType.DMA((3,)), pltpu.SemaphoreType.DMA((factor,)),
            pltpu.SemaphoreType.DMA((copies,)), pltpu.SemaphoreType.DMA((copies,)),
        ],
        compiler_params=pltpu.CompilerParams(collective_id=0, has_side_effects=True),
    )(trajectory, target, reaction, guess)


def solution(mesh):
    in_specs = (P("tm", "space", None), P("space", None), P("space", None), P("tm", "space", None))
    out_specs = P("tm", "space", None)
    return jax.shard_map(local, mesh=mesh, in_specs=in_specs, out_specs=out_specs, check_vma=False)
```

time: 216 us -> 30.2 us (0.14)
  waiting for transfers between devices: 138 us -> 0 us
  starting transfers between devices: 41.3 us -> 0 us
  Pallas kernels: 0 us -> 28.1 us
  other arithmetic: 21.4 us -> 0 us
  between operations: 13.8 us -> 0.01 us
    all_gather x2 -> x0, waiting for transfers between devices: 85.9 us -> none  [entering(): everything = jax.tree.map(lambda part: lax.all_gather(part, axis), x)]
    ppermute x25 -> x0, waiting for transfers between devices: 51 us -> none  [the longest x11 44.9 us: extended_2(): lax.ppermute(head, axis, [((i + 1) % count, i) for i in range(ends)])]
    ppermute x25 -> x0, starting transfers between devices: 41.2 us -> none  [the longest x11 23.1 us: extended_2(): lax.ppermute(tail, axis, [(i, (i + 1) % count) for i in range(ends)])]
    pallas_call x0 -> x1, Pallas kernels: none -> 28.1 us  [local(): pl.pallas_call(functools.partial(kernel, n, ns, size, float(factor * n)),...]
    select_n x16 -> x0, other arithmetic: 17.1 us -> none  [turn(): return jax.tree.map(lambda a, b: jnp.where(reached, a, b), new, before)]
  transfers between devices with their start and end apart: 27 -> 0, of which waited for: 16 -> 0; matrix products, arithmetic and copies ran while one was open for 1% -> 0% of each run, Pallas kernels for 0% -> 0%
where the time goes in v1:
time: 30.2 us; the launch traced here: 30 us
  Pallas kernels  28.1 us (93%)
  local copies, waits for them, and re-layouts  1.89 us (6%)
    pallas_call x1, Pallas kernels, local(): pl.pallas_call(functools.partial(kernel, n, ns, size, float(factor * n)),...  28.1 us
    unnamed x1, local copies, waits for them, and re-layouts  1.89 us

profile of v1, /device:TPU:0, one launch (start us, length us, event | category | flops | bytes accessed | tf_op | source)
XLA Modules:
  0.0 30.0 jit_solution(17374793895427121125)
XLA Ops:
  0.0 28.1 %shard_map.46 = f32[4,32,1024]{2,1,0:T(8,128)} custom-call(bf16[4,32,1024]{2,1,0:T(8,128)(2,1)} %traj_in.1, f32[32,1024]{1,0:T(8,128)} %targ_in.1, f32[32,1024]{1,0:T(8,128)} %reac_in.1, f32[1,32,1024]{2,1,0:T(8,128)} %guess_in.1), custom_call_target="tpu_custom_call" | custom-call | tf_op jit(solution)/shard_map/pallas_call | solution.py:294
  28.1 1.9 %copy.6 = f32[4,32,1024]{2,1,0:T(8,128)} copy(f32[4,32,1024]{2,1,0:T(8,128)} %shard_map.46) | data formatting | bytes 1048576

commit v2 on v1

--- a/solution.py
+++ b/solution.py
@@ -113,11 +113,25 @@
             Move(source, x, (t - 1, s), has_prev, has_next),
         ]
 
-    def part(k):
-        return pl.ds(pl.multiple_of(k * quarter, quarter), quarter)
+    def split(ref, value):
+        for k in range(size):
+            ref[k] = value[:, k * quarter : (k + 1) * quarter]
+
+    def joined(ref, *lead):
+        return jnp.concatenate([ref[(*lead, k)] for k in range(size)], 1)
 
     def member(d):
         return lax.rem(m + d, size)
+
+    def transpose(source, target):
+        moves = [
+            Move(source.at[member(d)], target.at[m], (base + member(d), s), always, always)
+            for d in range(1, size)
+        ]
+        for move in moves:
+            move.start()
+        target[m] = source[m]
+        return moves
 
     pl.semaphore_wait(barrier, greeted)
     first = to_previous(guess_in.at[0], x0, x0h)
@@ -159,7 +173,8 @@
     product = 1.0 + rates[0]
     for i in range(1, factor):
         product = product * (1.0 + rates[i])
-    arate[...] = product
+    split(arate, product)
+    a_moves = transpose(arate, ga)
     below = jnp.where(has_down, DIFFUSION, 0.0).astype(jnp.float32)
     above = jnp.where(has_up, DIFFUSION, 0.0).astype(jnp.float32)
     spread[...] = jnp.where(sub, below, above)
@@ -193,22 +208,10 @@
     for move in second:
         move.start()
 
-    def transpose(source, target):
-        moves = [
-            Move(source.at[:, part(member(d))], target.at[m], (base + member(d), s), always, always)
-            for d in range(1, size)
-        ]
-        for move in moves:
-            move.start()
-        target[m] = source[:, part(m)]
-        return moves
-
-    a_moves = transpose(arate, ga)
-
     for move in second:
         move.landed()
     centre = relax(jnp.concatenate([x1[...], halo(x1h[0], x1h[1])], 0))
-    res[...] = centre - c1[...]
+    split(res, centre - c1[...])
     r_moves = transpose(res, gr)
 
     def to_lower(source, target):
@@ -252,23 +255,23 @@
         k = member(d)
         to = base + k
         moves = [
-            Move(es.at[k, top], eh.at[0, :, part(m)], (to, s - 1), has_up, has_down),
-            Move(es.at[k, bottom], eh.at[1, :, part(m)], (to, s + 1), has_down, has_up),
+            Move(es.at[k, top], eh.at[0, m], (to, s - 1), has_up, has_down),
+            Move(es.at[k, bottom], eh.at[1, m], (to, s + 1), has_down, has_up),
         ]
         if d:
-            moves.append(Move(es.at[k], e.at[:, part(m)], (to, s), always, always))
+            moves.append(Move(es.at[k], e.at[m], (to, s), always, always))
         for move in moves:
             move.start()
         e_moves += moves
-    e[:, part(m)] = es[m]
+    e[m] = es[m]
     for move in e_moves:
         move.landed()
 
-    entering = e[...]
-    fine[0] = c1[...] + (arate[...] * entering + res[...])
+    entering = joined(e)
+    fine[0] = c1[...] + (joined(arate) * entering + joined(res))
     outs = [pltpu.make_async_copy(fine.at[i], out_ref.at[i], out_sem.at[i]) for i in range(factor)]
     outs[0].start()
-    v = jnp.concatenate([x1[...] + entering, halo(x1h[0], x1h[1]) + halo(eh[0], eh[1])], 0)
+    v = jnp.concatenate([x1[...] + entering, halo(x1h[0], x1h[1]) + halo(joined(eh, 0), joined(eh, 1))], 0)
     for i in range(factor - 1, 0, -1):
         v = advance(v, i)
         fine[i] = v[:rows]
@@ -300,14 +303,14 @@
             pltpu.VMEM((factor, rows, cols), trajectory.dtype),
             vmem(rows, cols), vmem(rows, cols),
             vmem(factor, ext, cols), vmem(factor, ext, cols), vmem(EDGE, cols),
-            vmem(rows, cols),
+            vmem(size, rows, quarter),
             vmem(rows, cols), vmem(2, EDGE, cols), vmem(rows, cols), vmem(2, EDGE, cols),
             vmem(factor - 1, 2, EDGE, cols), vmem(factor - 1, 2, EDGE, cols),
-            vmem(rows, cols), vmem(rows, cols),
+            vmem(rows, cols), vmem(size, rows, quarter),
             vmem(size, rows, quarter), vmem(size, rows, quarter),
             vmem(rows, quarter), vmem(rows, quarter),
             vmem(groups, rows, quarter), vmem(groups, rows, quarter),
-            vmem(size, rows, quarter), vmem(rows, cols), vmem(2, EDGE, cols),
+            vmem(size, rows, quarter), vmem(size, rows, quarter), vmem(2, size, EDGE, quarter),
             vmem(factor, rows, cols),
             pltpu.SemaphoreType.DMA((3,)), pltpu.SemaphoreType.DMA((factor,)),
             pltpu.SemaphoreType.DMA((copies,)), pltpu.SemaphoreType.DMA((copies,)),

time: 30.2 us -> 29.8 us (0.987)
    pallas_call x1, Pallas kernels: 28.1 us -> 27.8 us  [local(): pl.pallas_call(functools.partial(kernel, n, ns, size, float(factor * n)),...]
where the time goes in v2:
time: 29.8 us; the launch traced here: 29.6 us
  Pallas kernels  27.8 us (93%)
  local copies, waits for them, and re-layouts  1.89 us (6%)
    pallas_call x1, Pallas kernels, local(): pl.pallas_call(functools.partial(kernel, n, ns, size, float(factor * n)),...  27.8 us
    unnamed x1, local copies, waits for them, and re-layouts  1.89 us

profile of v2, /device:TPU:0, one launch (start us, length us, event | category | flops | bytes accessed | tf_op | source)
XLA Modules:
  0.0 29.6 jit_solution(4797180245691705421)
XLA Ops:
  0.0 27.8 %shard_map.46 = f32[4,32,1024]{2,1,0:T(8,128)} custom-call(bf16[4,32,1024]{2,1,0:T(8,128)(2,1)} %traj_in.1, f32[32,1024]{1,0:T(8,128)} %targ_in.1, f32[32,1024]{1,0:T(8,128)} %reac_in.1, f32[1,32,1024]{2,1,0:T(8,128)} %guess_in.1), custom_call_target="tpu_custom_call" | custom-call | tf_op jit(solution)/shard_map/pallas_call | solution.py:297
  27.8 1.9 %copy.6 = f32[4,32,1024]{2,1,0:T(8,128)} copy(f32[4,32,1024]{2,1,0:T(8,128)} %shard_map.46) | data formatting | bytes 1048576

commit v3 on v2

--- a/solution.py
+++ b/solution.py
@@ -24,7 +24,7 @@
     traj_in, targ_in, reac_in, guess_in, out_ref,
     traj, targ, reac, coef, src, spread, arate, x0, x0h, x1, x1h, packs, packr,
     c1, res, ga, gr, ppa, pp, rpa, rp, es, e, eh, fine,
-    load_sem, out_sem, send_sem, recv_sem,
+    load_sem, out_sem, send_sem, recv_sem, lower_sem,
 ):
     factor, rows, cols = traj.shape
     quarter = cols // size
@@ -77,9 +77,8 @@
             greeted += greet(here, (t, s + ds))
         for d in range(1, size):
             greeted += greet(here, (base + lax.rem(m + d, size), s + ds))
-    for d in range(1, groups):
-        greeted += greet(g - d >= 0, (t - d * size, s))
-        greeted += greet(g + d < groups, (t + d * size, s))
+    greeted += greet(g > 0, (t - size, s))
+    greeted += greet(g + 1 < groups, (t + size, s))
 
     counter = [0]
     sent = []
@@ -123,14 +122,15 @@
     def member(d):
         return lax.rem(m + d, size)
 
-    def transpose(source, target):
+    whole = pl.ds(0, rows)
+
+    def transpose(source, target, strip):
         moves = [
-            Move(source.at[member(d)], target.at[m], (base + member(d), s), always, always)
+            Move(source.at[member(d), strip], target.at[m, strip], (base + member(d), s), always, always)
             for d in range(1, size)
         ]
         for move in moves:
             move.start()
-        target[m] = source[m]
         return moves
 
     pl.semaphore_wait(barrier, greeted)
@@ -174,7 +174,8 @@
     for i in range(1, factor):
         product = product * (1.0 + rates[i])
     split(arate, product)
-    a_moves = transpose(arate, ga)
+    a_moves = transpose(arate, ga, whole)
+    ga[m] = arate[m]
     below = jnp.where(has_down, DIFFUSION, 0.0).astype(jnp.float32)
     above = jnp.where(has_up, DIFFUSION, 0.0).astype(jnp.float32)
     spread[...] = jnp.where(sub, below, above)
@@ -208,15 +209,27 @@
     for move in second:
         move.start()
 
+    @pl.when(g > 1)
+    def _():
+        pl.semaphore_wait(lower_sem, 1)
+
+    @pl.when(both(g > 0, g + 1 < groups))
+    def _():
+        pl.semaphore_signal(lower_sem, inc=1, device_id=(t + size, s), device_id_type=MESH)
+
     for move in second:
         move.landed()
     centre = relax(jnp.concatenate([x1[...], halo(x1h[0], x1h[1])], 0))
     split(res, centre - c1[...])
-    r_moves = transpose(res, gr)
-
-    def to_lower(source, target):
+    count = rows // EDGE
+    chunks = [0, count - 1] + list(range(1, count - 1)) if count > 1 else [0]
+    strip = {c: pl.ds(c * EDGE, EDGE) for c in chunks}
+    r_moves = {c: transpose(res, gr, strip[c]) for c in chunks}
+    gr[m] = res[m]
+
+    def to_lower(source, target, strip):
         moves = [
-            Move(source, target.at[d], (t - d * size, s), g - d >= 0, g + d < groups)
+            Move(source.at[strip], target.at[d, strip], (t - d * size, s), g - d >= 0, g + d < groups)
             for d in range(groups - 1, 0, -1)
         ]
         for move in moves:
@@ -229,40 +242,44 @@
     for k in range(1, size):
         value = value * ga[k]
     ppa[...] = value
-    pa_moves = to_lower(ppa, rpa)
-
-    for move in r_moves:
-        move.landed()
-    value = gr[size - 1]
-    for k in range(size - 2, -1, -1):
-        value = ga[k] * value + gr[k]
-    pp[...] = value
-    p_moves = to_lower(pp, rp)
+    pa_moves = to_lower(ppa, rpa, whole)
+
+    p_moves = {}
+    for c in chunks:
+        for move in r_moves[c]:
+            move.landed()
+        value = gr[size - 1, strip[c]]
+        for k in range(size - 2, -1, -1):
+            value = ga[k, strip[c]] * value + gr[k, strip[c]]
+        pp[strip[c]] = value
+        p_moves[c] = to_lower(pp, rp, strip[c])
     for move in pa_moves:
         move.landed()
-    for move in p_moves:
-        move.landed()
-
-    value = rp[groups - 1]
-    for d in range(groups - 2, 0, -1):
-        value = rp[d] + rpa[d] * value
-    es[size - 1] = value
-    for k in range(size - 1, 0, -1):
-        value = ga[k] * value + gr[k]
-        es[k - 1] = value
+
     e_moves = []
-    for d in range(size - 1, -1, -1):
-        k = member(d)
-        to = base + k
-        moves = [
-            Move(es.at[k, top], eh.at[0, m], (to, s - 1), has_up, has_down),
-            Move(es.at[k, bottom], eh.at[1, m], (to, s + 1), has_down, has_up),
-        ]
-        if d:
-            moves.append(Move(es.at[k], e.at[m], (to, s), always, always))
-        for move in moves:
-            move.start()
-        e_moves += moves
+    for c in chunks:
+        for move in p_moves[c]:
+            move.landed()
+        value = rp[groups - 1, strip[c]]
+        for d in range(groups - 2, 0, -1):
+            value = rp[d, strip[c]] + rpa[d, strip[c]] * value
+        es[size - 1, strip[c]] = value
+        for k in range(size - 1, 0, -1):
+            value = ga[k, strip[c]] * value + gr[k, strip[c]]
+            es[k - 1, strip[c]] = value
+        for d in range(size):
+            k = member(d)
+            to = base + k
+            moves = []
+            if c == 0:
+                moves.append(Move(es.at[k, top], eh.at[0, m], (to, s - 1), has_up, has_down))
+            if c == count - 1:
+                moves.append(Move(es.at[k, bottom], eh.at[1, m], (to, s + 1), has_down, has_up))
+            if d:
+                moves.append(Move(es.at[k, strip[c]], e.at[m, strip[c]], (to, s), always, always))
+            for move in moves:
+                move.start()
+            e_moves += moves
     e[m] = es[m]
     for move in e_moves:
         move.landed()
@@ -290,7 +307,8 @@
     groups = n // size
     quarter = cols // size
     ext = rows + EDGE
-    copies = 6 + 2 * (factor - 1) + 2 * (size - 1) + 2 * (groups - 1) + 3 * size - 1
+    count = rows // EDGE
+    copies = 6 + 2 * (factor - 1) + (2 * count + 1) * (size - 1) + (count + 1) * (groups - 1) + 2 * size
     f32 = jnp.float32
     vmem = lambda *shape: pltpu.VMEM(shape, f32)
     anywhere = pl.BlockSpec(memory_space=pl.ANY)
@@ -314,6 +332,7 @@
             vmem(factor, rows, cols),
             pltpu.SemaphoreType.DMA((3,)), pltpu.SemaphoreType.DMA((factor,)),
             pltpu.SemaphoreType.DMA((copies,)), pltpu.SemaphoreType.DMA((copies,)),
+            pltpu.SemaphoreType.REGULAR,
         ],
         compiler_params=pltpu.CompilerParams(collective_id=0, has_side_effects=True),
     )(trajectory, target, reaction, guess)

time: 29.8 us -> 29.5 us (0.990)
  Pallas kernels: 27.8 us -> 27.4 us
    pallas_call x1, Pallas kernels: 27.8 us -> 27.4 us  [local(): pl.pallas_call(functools.partial(kernel, n, ns, size, float(factor * n)),...]
where the time goes in v3:
time: 29.5 us; the launch traced here: 29.3 us
  Pallas kernels  27.4 us (93%)
  local copies, waits for them, and re-layouts  1.89 us (6%)
    pallas_call x1, Pallas kernels, local(): pl.pallas_call(functools.partial(kernel, n, ns, size, float(factor * n)),...  27.4 us
    unnamed x1, local copies, waits for them, and re-layouts  1.89 us

profile of v3, /device:TPU:0, one launch (start us, length us, event | category | flops | bytes accessed | tf_op | source)
XLA Modules:
  0.0 29.3 jit_solution(6646554345627646153)
XLA Ops:
  0.0 27.4 %shard_map.46 = f32[4,32,1024]{2,1,0:T(8,128)} custom-call(bf16[4,32,1024]{2,1,0:T(8,128)(2,1)} %traj_in.1, f32[32,1024]{1,0:T(8,128)} %targ_in.1, f32[32,1024]{1,0:T(8,128)} %reac_in.1, f32[1,32,1024]{2,1,0:T(8,128)} %guess_in.1), custom_call_target="tpu_custom_call" | custom-call | tf_op jit(solution)/shard_map/pallas_call | solution.py:315
  27.4 1.9 %copy.6 = f32[4,32,1024]{2,1,0:T(8,128)} copy(f32[4,32,1024]{2,1,0:T(8,128)} %shard_map.46) | data formatting | bytes 1048576

commit v4 on v3

--- a/solution.py
+++ b/solution.py
@@ -19,12 +19,40 @@
     return best
 
 
+def advance(v, i, coef, src, spread):
+    ext, cols = v.shape
+    rows = ext - EDGE
+    column = lax.broadcasted_iota(jnp.int32, (ext, cols), 1)
+    around = pltpu.roll(v, 1, 0) + pltpu.roll(v, ext - 1, 0)
+    around = around + jnp.where(column == 0, 0.0, pltpu.roll(v, 1, 1))
+    around = around + jnp.where(column == cols - 1, 0.0, pltpu.roll(v, cols - 1, 1))
+    scaled = jnp.concatenate([DIFFUSION * around[:rows], spread[...] * around[rows:]], 0)
+    return coef[i] * v + scaled + src[i]
+
+
+def finish(coef, src, spread, last, c2, out_ref, fine, out_sem):
+    factor, ext, _ = coef.shape
+    rows = ext - EDGE
+    outs = [
+        pltpu.make_async_copy(fine.at[i] if i else c2, out_ref.at[i], out_sem.at[i])
+        for i in range(factor)
+    ]
+    outs[0].start()
+    v = last[...]
+    for i in range(factor - 1, 0, -1):
+        v = advance(v, i, coef, src, spread)
+        fine[i] = v[:rows]
+        outs[i].start()
+    for copy in outs:
+        copy.wait()
+
+
 def kernel(
     n, ns, size, steps,
-    traj_in, targ_in, reac_in, guess_in, out_ref,
-    traj, targ, reac, coef, src, spread, arate, x0, x0h, x1, x1h, packs, packr,
-    c1, res, ga, gr, ppa, pp, rpa, rp, es, e, eh, fine,
-    load_sem, out_sem, send_sem, recv_sem, lower_sem,
+    traj_in, targ_in, reac_in, guess_in, coef, src, spread, last, c2,
+    traj, targ, reac, arate, x0, x0h, x1, x1h, packs, packr,
+    c1, res, ga, gr, ppa, pp, rpa, rp, es, e, eh,
+    load_sem, send_sem, recv_sem, lower_sem,
 ):
     factor, rows, cols = traj.shape
     quarter = cols // size
@@ -187,18 +215,9 @@
         coef[i, rows:] = halo(b, a)
         src[i, rows:] = pltpu.roll(halo(a, b), half, 0)
 
-    column = lax.broadcasted_iota(jnp.int32, (ext, cols), 1)
-
-    def advance(v, i):
-        around = pltpu.roll(v, 1, 0) + pltpu.roll(v, ext - 1, 0)
-        around = around + jnp.where(column == 0, 0.0, pltpu.roll(v, 1, 1))
-        around = around + jnp.where(column == cols - 1, 0.0, pltpu.roll(v, cols - 1, 1))
-        scaled = jnp.concatenate([DIFFUSION * around[:rows], spread[...] * around[rows:]], 0)
-        return coef[i] * v + scaled + src[i]
-
     def relax(v):
         for i in range(factor - 1, -1, -1):
-            v = advance(v, i)
+            v = advance(v, i, coef, src, spread)
         return v[:rows]
 
     for move in first:
@@ -285,16 +304,9 @@
         move.landed()
 
     entering = joined(e)
-    fine[0] = c1[...] + (joined(arate) * entering + joined(res))
-    outs = [pltpu.make_async_copy(fine.at[i], out_ref.at[i], out_sem.at[i]) for i in range(factor)]
-    outs[0].start()
-    v = jnp.concatenate([x1[...] + entering, halo(x1h[0], x1h[1]) + halo(joined(eh, 0), joined(eh, 1))], 0)
-    for i in range(factor - 1, 0, -1):
-        v = advance(v, i)
-        fine[i] = v[:rows]
-        outs[i].start()
-    for copy in outs:
-        copy.wait()
+    c2[...] = c1[...] + (joined(arate) * entering + joined(res))
+    last[:rows] = x1[...] + entering
+    last[rows:] = halo(x1h[0], x1h[1]) + halo(joined(eh, 0), joined(eh, 1))
     for move in sent:
         move.left()
 
@@ -311,16 +323,19 @@
     copies = 6 + 2 * (factor - 1) + (2 * count + 1) * (size - 1) + (count + 1) * (groups - 1) + 2 * size
     f32 = jnp.float32
     vmem = lambda *shape: pltpu.VMEM(shape, f32)
-    anywhere = pl.BlockSpec(memory_space=pl.ANY)
-    return pl.pallas_call(
+    resident = pl.BlockSpec(memory_space=pltpu.VMEM)
+    shape = lambda *dims: jax.ShapeDtypeStruct(dims, f32)
+    parts = pl.pallas_call(
         functools.partial(kernel, n, ns, size, float(factor * n)),
-        out_shape=jax.ShapeDtypeStruct((factor, rows, cols), f32),
-        in_specs=[anywhere] * 4,
-        out_specs=anywhere,
+        out_shape=[
+            shape(factor, ext, cols), shape(factor, ext, cols), shape(EDGE, cols),
+            shape(ext, cols), shape(rows, cols),
+        ],
+        in_specs=[pl.BlockSpec(memory_space=pltpu.HBM)] * 4,
+        out_specs=[resident] * 5,
         scratch_shapes=[
             pltpu.VMEM((factor, rows, cols), trajectory.dtype),
             vmem(rows, cols), vmem(rows, cols),
-            vmem(factor, ext, cols), vmem(factor, ext, cols), vmem(EDGE, cols),
             vmem(size, rows, quarter),
             vmem(rows, cols), vmem(2, EDGE, cols), vmem(rows, cols), vmem(2, EDGE, cols),
             vmem(factor - 1, 2, EDGE, cols), vmem(factor - 1, 2, EDGE, cols),
@@ -329,13 +344,22 @@
             vmem(rows, quarter), vmem(rows, quarter),
             vmem(groups, rows, quarter), vmem(groups, rows, quarter),
             vmem(size, rows, quarter), vmem(size, rows, quarter), vmem(2, size, EDGE, quarter),
-            vmem(factor, rows, cols),
-            pltpu.SemaphoreType.DMA((3,)), pltpu.SemaphoreType.DMA((factor,)),
+            pltpu.SemaphoreType.DMA((3,)),
             pltpu.SemaphoreType.DMA((copies,)), pltpu.SemaphoreType.DMA((copies,)),
             pltpu.SemaphoreType.REGULAR,
         ],
-        compiler_params=pltpu.CompilerParams(collective_id=0, has_side_effects=True),
-    )(trajectory, target, reaction, guess)
+        compiler_params=pltpu.CompilerParams(
+            collective_id=0, has_side_effects=True, vmem_limit_bytes=16 << 20
+        ),
+    )(*[pltpu.with_memory_space_constraint(x, pltpu.HBM) for x in (trajectory, target, reaction, guess)])
+    return pl.pallas_call(
+        finish,
+        out_shape=shape(factor, rows, cols),
+        in_specs=[resident] * 5,
+        out_specs=pl.BlockSpec(memory_space=pltpu.HBM),
+        scratch_shapes=[vmem(factor, rows, cols), pltpu.SemaphoreType.DMA((factor,))],
+        compiler_params=pltpu.CompilerParams(vmem_limit_bytes=16 << 20),
+    )(*parts)
 
 
 def solution(mesh):

time: 29.5 us -> 27.6 us (0.936)
  local copies, waits for them, and re-layouts: 1.89 us -> 0 us
    unnamed x1 -> x0, local copies, waits for them, and re-layouts: 1.89 us -> none
    pallas_call x0 -> x1, Pallas kernels: none -> 1.1 us  [local(): pl.pallas_call(finish, out_shape=shape(factor, rows, cols), in_specs=[res...]
    pallas_call x1, Pallas kernels: 27.4 us -> 26.4 us  [local(): pl.pallas_call(functools.partial(kernel, n, ns, size, float(factor * n)),...]
where the time goes in v4:
time: 27.6 us; the launch traced here: 27.5 us
  Pallas kernels  27.5 us (100%)
    pallas_call x1, Pallas kernels, local(): pl.pallas_call(functools.partial(kernel, n, ns, size, float(factor * n)),...  26.4 us
    pallas_call x1, Pallas kernels, local(): pl.pallas_call(finish, out_shape=shape(factor, rows, cols), in_specs=[res...  1.1 us

profile of v4, /device:TPU:0, one launch (start us, length us, event | category | flops | bytes accessed | tf_op | source)
XLA Modules:
  0.0 27.5 jit_solution(15353977115916812177)
XLA Ops:
  0.0 26.4 %shard_map.46 = (f32[4,40,1024]{2,1,0:T(8,128)S(1)}, f32[4,40,1024]{2,1,0:T(8,128)S(1)}, f32[8,1024]{1,0:T(8,128)S(1)}, f32[40,1024]{1,0:T(8,128)S(1)}, f32[32,1024]{1,0:T(8,128)S(1)}) custom-call(bf16[4,32,1024]{2,1,0:T(8,128)(2,1)} %traj_in.1, f32[32,1024]{1,0:T(8,128)} %targ_in.1, f32[32,1024]{1,0:T(8,128)} %reac_in.1, f32[1,32,1024]{2,1,0:T(8,128)} %guess_in.1), custom_call_target="tpu_custom_call" | custom-call | tf_op jit(solution)/shard_map/pallas_call | solution.py:328
  26.4 1.1 %shard_map.47 = f32[4,32,1024]{2,1,0:T(8,128)} custom-call(f32[4,40,1024]{2,1,0:T(8,128)S(1)} %get-tuple-element.10.coef, f32[4,40,1024]{2,1,0:T(8,128)S(1)} %get-tuple-element.11.src, f32[8,1024]{1,0:T(8,128)S(1)} %get-tuple-element.12.spread, f32[40,1024]{1,0:T(8,128)S(1)} %get-tuple-element.13.last, f32[32,1024]{1,0:T(8,128)S(1)} %get-tuple-element.14.c2), custom_call_target="tpu_custom_call" | custom-call | tf_op jit(solution)/shard_map/pallas_call | solution.py:355
